TPU v7x, 128 devices: a whole 4x4x4 slice. The times are simulated.
128 devices in a mesh: layer: 4 (over z_lo, core), row: 8 (over z_hi, y), col: 4 (over x).
Axes of the slice: x: 4, y: 4, z: 4 (z_hi: 2, z_lo: 2; z = z_hi * 2 + z_lo), core: 2. Of those that a mesh axis runs over, the one named last changes fastest.
Arguments:
- grad: bfloat16 [32768, 8192], P(('layer', 'row'), 'col'), parts along dimension 0, may hold values from -6 to 6
- error: bfloat16 [32768, 8192], P(('layer', 'row'), 'col'), parts along dimension 0, may hold values from -2 to 2
- left_old: bfloat16 [32768, 512], P(('layer', 'row')), parts along dimension 0, may hold values from -0.25 to 0.25
- right_old: bfloat16 [32768, 512], P(('layer', 'col')), parts along dimension 0, may hold values from -0.25 to 0.25
- first_old: float32 [2048, 512], P('layer'), parts along dimension 0, may hold values from -3 to 3
- second_old: float32 [2048, 512], P('layer'), parts along dimension 0, may hold values from 0.05 to 1
Outputs:
- error_new: bfloat16 [32768, 8192], P(('layer', 'row'), 'col'), parts along dimension 0
- first_moment: float32 [2048, 512], P('layer'), parts along dimension 0
- second_moment: float32 [2048, 512], P('layer'), parts along dimension 0
- update: float32 [2048, 512], P('layer'), parts along dimension 0
There are 4 independent parts, one for each index of `layer`. A program takes and returns all parts, laid end to end along the dimension named above; each array names one. Nothing has to cross between parts.
All inputs are finite; a program needn't handle non-finite values.
Results may differ from a plain program's by a relative error of at most 0.0075.
Values may be sent and summed in bfloat16 or wider, within the bound.
No kernel may reach another device: no remote copies, remote signals or barrier semaphores. Data moves between devices by JAX's collectives and lax.ppermute only.
A program may use at most 128 MiB of HBM per device.

v0:
```python
import jax
import jax.numpy as jnp
from jax import lax
from jax.sharding import PartitionSpec as P


def solve_rows(image, gram):
    factor = jnp.linalg.cholesky(gram)
    return jax.scipy.linalg.solve_triangular(factor, image.T, lower=True).T.astype(jnp.bfloat16)


def gram_of(image):
    return lax.dot_general(image, image, (((0,), (0,)), ((), ())), precision=lax.Precision.HIGH)


def split_pair(values):
    upper = values.astype(jnp.bfloat16)
    lower = (values - upper.astype(jnp.float32)).astype(jnp.bfloat16)
    return (upper, lower)


def per_device(grad, error, left_old, right_old, first_old, second_old):
    highest = lax.Precision.HIGHEST
    across = (((0,), (0,)), ((), ()))
    left_image = lax.psum(jnp.dot(grad, right_old, preferred_element_type=jnp.float32), "col")
    left_gram = lax.psum(gram_of(left_image), "row")
    left_basis = solve_rows(left_image, left_gram)
    right_part = lax.dot_general(grad, left_basis, across, preferred_element_type=jnp.float32)
    right_image = lax.psum(right_part, "row")
    right_gram = lax.psum(gram_of(right_image), "col")
    right_basis = solve_rows(right_image, right_gram)
    summed = grad.astype(jnp.float32) + error.astype(jnp.float32)
    accum = summed.astype(jnp.bfloat16)
    carried = jnp.dot(accum, right_basis, preferred_element_type=jnp.float32)
    carried_upper, carried_lower = split_pair(carried)
    core_part = lax.dot_general(
        left_basis, carried_upper, across, preferred_element_type=jnp.float32
    ) + lax.dot_general(left_basis, carried_lower, across, preferred_element_type=jnp.float32)
    left_count = left_basis.shape[0] // lax.axis_size("col")
    left_start = lax.axis_index("col") * left_count
    left_piece = lax.dynamic_slice_in_dim(left_basis, left_start, left_count, 0)
    left_prior = lax.dynamic_slice_in_dim(left_old, left_start, left_count, 0)
    right_count = right_basis.shape[0] // lax.axis_size("row")
    right_start = lax.axis_index("row") * right_count
    right_piece = lax.dynamic_slice_in_dim(right_basis, right_start, right_count, 0)
    right_prior = lax.dynamic_slice_in_dim(right_old, right_start, right_count, 0)
    turn_left_part = lax.dot_general(
        left_piece, left_prior, across, preferred_element_type=jnp.float32
    )
    turn_right_part = lax.dot_general(
        right_piece, right_prior, across, preferred_element_type=jnp.float32
    )
    core, turn_left, turn_right = lax.psum(
        (core_part, turn_left_part, turn_right_part), ("row", "col")
    )
    core_upper, core_lower = split_pair(core)
    lifted_full = jnp.dot(left_basis, core_upper, preferred_element_type=jnp.float32) + jnp.dot(
        left_basis, core_lower, preferred_element_type=jnp.float32
    )
    lifted = lifted_full.astype(jnp.bfloat16)
    rebuilt = lax.dot_general(
        lifted, right_basis, (((1,), (1,)), ((), ())), preferred_element_type=jnp.float32
    )
    error_new = (summed - rebuilt).astype(jnp.bfloat16)
    first_turned = jnp.dot(
        jnp.dot(turn_left, first_old, precision=highest), turn_right.T, precision=highest
    )
    excess = jnp.maximum(second_old - first_old * first_old, 0.0)
    second_turned = (
        jnp.dot(
            jnp.dot(turn_left * turn_left, excess, precision=highest),
            (turn_right * turn_right).T,
            precision=highest,
        )
        + first_turned * first_turned
    )
    first_moment = 0.9 * first_turned + 0.1 * core
    second_moment = 0.999 * second_turned + 0.001 * core * core
    update = first_moment / (jnp.sqrt(second_moment) + 0.01)
    return (error_new, first_moment, second_moment, update)


def solution(mesh):
    return jax.shard_map(
        per_device,
        mesh=mesh,
        in_specs=(
            P(("layer", "row"), "col"),
            P(("layer", "row"), "col"),
            P(("layer", "row"), None),
            P(("layer", "col"), None),
            P("layer", None),
            P("layer", None),
        ),
        out_specs=(
            P(("layer", "row"), "col"),
            P("layer", None),
            P("layer", None),
            P("layer", None),
        ),
        check_vma=False,
    )
```

profile of v0, /device:TPU:0, one launch (start us, length us, event | category | flops | bytes accessed | tf_op | source)
XLA Modules:
  0.0 1060.0 jit_solution(5173255046993698777)
XLA Ops:
  7.2 1.5 copy-done
  8.8 5.8 fusion.102
  14.7 61.2 %all-reduce.8.cloned.1.call-done = f32[1024,512]{1,0:T(8,128)} async-done(((f32[1024,512]{1,0:T(8,128)}), f32[1024,512]{1,0:T(8,128)}) %all-reduce.8.cloned.1.call-update) | async-done | bytes 2097168 | tf_op jit(solution)/shard_map/psum | solution.py:25
  75.9 5.0 fusion.103
  81.4 87.5 %all-reduce.10.cloned.1.call-done = f32[512,512]{0,1:T(8,128)} async-done(((f32[512,512]{0,1:T(8,128)}), f32[512,512]{0,1:T(8,128)}) %all-reduce.10.cloned.1.call-update) | async-done | bytes 1048592 | tf_op jit(solution)/shard_map/psum | solution.py:26
  168.9 2.6 copy.11
  171.5 1.4 fusion.32
  174.0 11.7 %cholesky.286 = f32[128,128]{1,0:T(8,128)S(1)} custom-call(f32[128,128]{1,0:T(8,128)S(1)} %cholesky.426), custom_call_target="Cholesky" | custom-call | tf_op jit(solution)/shard_map/jit(cholesky)/cholesky | solution.py:8
  185.8 9.8 custom-call.33
  196.9 1.3 convolution_subtract_fusion.5
  198.2 11.7 %cholesky.305 = f32[128,128]{1,0:T(8,128)S(1)} custom-call(f32[128,128]{1,0:T(8,128)S(1)} %cholesky.430), custom_call_target="Cholesky" | custom-call | tf_op jit(solution)/shard_map/jit(cholesky)/cholesky | solution.py:8
  209.9 10.0 custom-call.34
  220.2 1.3 convolution_subtract_fusion.7
  221.5 11.7 %cholesky.326 = f32[128,128]{1,0:T(8,128)S(1)} custom-call(f32[128,128]{1,0:T(8,128)S(1)} %cholesky.435), custom_call_target="Cholesky" | custom-call | tf_op jit(solution)/shard_map/jit(cholesky)/cholesky | solution.py:8
  233.2 9.8 custom-call.35
  244.5 11.7 %cholesky.343 = f32[128,128]{1,0:T(8,128)S(1)} custom-call(f32[128,128]{1,0:T(8,128)S(1)} %convolution_subtract_fusion.9), custom_call_target="Cholesky" | custom-call | tf_op jit(solution)/shard_map/jit(cholesky)/cholesky | solution.py:8
  260.6 1.5 select_select_fusion.1
  262.1 11.6 %while.2 = (s32[]{:T(128)}, f32[512,512]{1,0:T(8,128)}, s32[4,2]{0,1:T(2,128)S(1)}, f32[4,128,128]{2,1,0:T(8,128)S(1)}, s32[]{:T(128)}) while((s32[]{:T(128)}, f32[512,512]{1,0:T(8,128)}, s32[4,2]{0,1:T(2,128)S(1)}, f32[4,128,128]{2,1,0:T(8,128)S(1)}, s32[]{:T(128)}) %tuple.61), condition=%wide.while_cond, body=%wide.while_body.sunk | while | flops 2 | bytes 131189 | solution.py:9
  262.7 2.3 bitcast_dynamic-update-slice_fusion.4
  265.6 2.3 bitcast_dynamic-update-slice_fusion.4
  268.5 2.3 bitcast_dynamic-update-slice_fusion.4
  271.5 2.2 bitcast_dynamic-update-slice_fusion.4
  273.7 39.3 %custom-call.28 = f32[4,128,128]{1,2,0:T(8,128)S(1)} custom-call(f32[4,128,128]{2,1,0:T(8,128)S(1)} %get-tuple-element.12), custom_call_target="InvertDiagBlocksLowerTriangular" | custom-call | tf_op jit(solution)/shard_map/jit(_solve_triangular)/triangular_solve | solution.py:9
  313.0 1.8 fusion.98
  314.9 2.2 convolution_subtract_fusion.3
  317.7 2.8 convolution_subtract_fusion.2
  321.2 4.0 fusion.23
  325.9 4.4 convolution_bitcast_fusion
  330.4 108.0 %all-reduce.12.cloned.1.call-done = f32[2048,512]{0,1:T(8,128)} async-done(((f32[2048,512]{0,1:T(8,128)}), f32[2048,512]{0,1:T(8,128)}) %all-reduce.12.cloned.1.call-update) | async-done | bytes 4194320 | tf_op jit(solution)/shard_map/psum | solution.py:29
  438.3 7.9 fusion.104
  446.6 2.2 fusion.50
  448.8 42.1 %all-reduce.14.cloned.1.call-done = f32[512,512]{0,1:T(8,128)} async-done(((f32[512,512]{0,1:T(8,128)}), f32[512,512]{0,1:T(8,128)}) %all-reduce.14.cloned.1.call-update) | async-done | bytes 1048592 | tf_op jit(solution)/shard_map/psum | solution.py:30
  490.9 2.6 copy.13
  493.5 1.4 fusion.31
  496.0 11.7 %cholesky.358 = f32[128,128]{1,0:T(8,128)S(1)} custom-call(f32[128,128]{1,0:T(8,128)S(1)} %cholesky.439), custom_call_target="Cholesky" | custom-call | tf_op jit(solution)/shard_map/jit(cholesky)/cholesky | solution.py:8
  507.9 9.8 custom-call.36
  520.9 11.7 %cholesky.377 = f32[128,128]{1,0:T(8,128)S(1)} custom-call(f32[128,128]{1,0:T(8,128)S(1)} %cholesky.443), custom_call_target="Cholesky" | custom-call | tf_op jit(solution)/shard_map/jit(cholesky)/cholesky | solution.py:8
  532.6 10.2 custom-call.37
  544.0 1.3 convolution_subtract_fusion.6
  545.9 13.2 %cholesky.398 = f32[128,128]{1,0:T(8,128)} custom-call(f32[128,128]{1,0:T(8,128)} %cholesky.448), custom_call_target="Cholesky" | custom-call | tf_op jit(solution)/shard_map/jit(cholesky)/cholesky | solution.py:8
  559.1 1.5 select_reduce_fusion.1
  560.6 11.3 %custom-call.38 = f32[1,128,128]{1,2,0:T(8,128)} custom-call(f32[1,128,128]{2,1,0:T(8,128)} %get-tuple-element.49), custom_call_target="InvertDiagBlocksLowerTriangular" | custom-call | tf_op jit(solution)/shard_map/jit(cholesky)/cholesky | solution.py:8
  574.1 11.9 %cholesky.415 = f32[128,128]{1,0:T(8,128)S(1)} custom-call(f32[128,128]{1,0:T(8,128)S(1)} %convolution_subtract_fusion.8), custom_call_target="Cholesky" | custom-call | tf_op jit(solution)/shard_map/jit(cholesky)/cholesky | solution.py:8
  592.2 11.6 %while.3 = (s32[]{:T(128)}, f32[512,512]{1,0:T(8,128)}, s32[4,2]{0,1:T(2,128)S(1)}, f32[4,128,128]{2,1,0:T(8,128)S(1)}, s32[]{:T(128)}) while((s32[]{:T(128)}, f32[512,512]{1,0:T(8,128)}, s32[4,2]{0,1:T(2,128)S(1)}, f32[4,128,128]{2,1,0:T(8,128)S(1)}, s32[]{:T(128)}) %tuple.78), condition=%wide.while_cond.1, body=%wide.while_body.1.sunk | while | flops 2 | bytes 131189 | solution.py:9
  592.8 2.3 bitcast_dynamic-update-slice_fusion.5
  595.7 2.3 bitcast_dynamic-update-slice_fusion.5
  598.6 2.3 bitcast_dynamic-update-slice_fusion.5
  601.5 2.2 bitcast_dynamic-update-slice_fusion.5
  603.8 39.3 %custom-call.29 = f32[4,128,128]{1,2,0:T(8,128)S(1)} custom-call(f32[4,128,128]{2,1,0:T(8,128)S(1)} %get-tuple-element.20), custom_call_target="InvertDiagBlocksLowerTriangular" | custom-call | tf_op jit(solution)/shard_map/jit(_solve_triangular)/triangular_solve | solution.py:9
  643.1 2.3 fusion.101
  645.4 2.5 convolution_subtract_fusion.1
  649.0 2.3 convolution_subtract_fusion
  652.4 3.2 fusion.9
  657.4 1.6 copy-done.23
  659.0 2.4 fusion.1
  662.1 1.7 convolution_add_fusion.1
  663.8 1.3 fusion.47
  665.1 362.9 %all-reduce.16.cloned.1.call-done = (f32[512,512]{1,0:T(8,128)}, f32[512,512]{1,0:T(8,128)}, f32[512,512]{1,0:T(8,128)}) async-done(((f32[512,512]{1,0:T(8,128)}, f32[512,512]{1,0:T(8,128)}, f32[512,512]{1,0:T(8,128)}), (f32[512,512]{1,0:T(8,128)}, f32[512,512]{1,0:T(8,128)}, f32[512,512]{1,0:T(8,128)})) %all-reduce.16.cloned.1.call-update) | async-done | bytes 3145744 | tf_op jit(solution)/shard_map/psum | solution.py:53
  1028.0 3.5 fusion.55
  1031.6 10.4 subtract_convert_fusion
  1042.0 3.2 fusion.105
  1045.3 2.0 fusion.34
  1047.3 1.9 fusion.106
  1049.1 4.1 add_divide_fusion
  (121 shorter events, 30.6 us)
Async XLA Ops:
  7.2 1.6 copy-start
  7.2 68.7 %all-reduce.8.cloned.1.call-start = ((), (), s32[]{:S(2)}) async-start(), calls=%async_computation | async-start | bytes 4194304 | tf_op jit(solution)/shard_map/psum | solution.py:25
  14.6 154.3 %all-reduce.10.cloned.1.call-start = ((), (), s32[]{:S(2)}) async-start(), calls=%async_computation.1 | async-start | bytes 2097152 | tf_op jit(solution)/shard_map/psum | solution.py:26
  80.9 357.4 %all-reduce.12.cloned.1.call-start = ((), (), s32[]{:S(2)}) async-start(), calls=%async_computation.2 | async-start | bytes 8388608 | tf_op jit(solution)/shard_map/psum | solution.py:29
  168.9 2.6 copy-start.5
  173.0 1.0 copy-start.8
  313.0 4.7 copy-start.2
  314.9 131.6 %copy-start.16 = (bf16[128,1024]{1,0:T(8,128)(2,1)}, bf16[128,1024]{1,0:T(8,128)(2,1)S(1)}, u32[]{:S(2)}) copy-start(bf16[128,1024]{1,0:T(8,128)(2,1)S(1)} %get-tuple-element.72) | copy-start | bytes 786436
  317.7 128.8 %copy-start.18 = (bf16[128,1024]{1,0:T(8,128)(2,1)}, bf16[128,1024]{1,0:T(8,128)(2,1)S(1)}, u32[]{:S(2)}) copy-start(bf16[128,1024]{1,0:T(8,128)(2,1)S(1)} %get-tuple-element.70) | copy-start | bytes 786436
  320.5 5.3 copy-start.24
  321.2 125.3 %copy-start.20 = (bf16[128,1024]{1,0:T(8,128)(2,1)}, bf16[128,1024]{1,0:T(8,128)(2,1)S(1)}, u32[]{:S(2)}) copy-start(bf16[128,1024]{1,0:T(8,128)(2,1)S(1)} %get-tuple-element.68) | copy-start | bytes 786436
  330.3 160.6 %all-reduce.14.cloned.1.call-start = ((), (), s32[]{:S(2)}) async-start(), calls=%async_computation.3 | async-start | bytes 2097152 | tf_op jit(solution)/shard_map/psum | solution.py:30
  446.2 581.8 %all-reduce.16.cloned.1.call-start = ((), (), s32[]{:S(2)}) async-start(), calls=%async_computation.4 | async-start | bytes 6291456 | tf_op jit(solution)/shard_map/psum | solution.py:53
  490.9 2.6 copy-start.4
  495.0 1.0 copy-start.9
  520.2 0.7 copy-start.22
  645.4 11.5 %copy-start.11 = (bf16[128,2048]{1,0:T(8,128)(2,1)}, bf16[128,2048]{1,0:T(8,128)(2,1)S(1)}, u32[]{:S(2)}) copy-start(bf16[128,2048]{1,0:T(8,128)(2,1)S(1)} %get-tuple-element.80) | copy-start | bytes 1572868
  645.4 3.6 copy-start.1
  648.9 7.9 copy-start.12
  652.3 4.6 copy-start.13
  652.3 5.1 copy-start.25
  656.6 0.8 copy-start.10
  656.6 2.4 copy-start.23
  659.0 2.4 copy-start.17
  659.0 2.4 copy-start.19
  659.0 2.4 copy-start.21
  1031.6 10.5 copy-start.6
  1042.0 3.2 copy-start.7
  1042.0 3.2 copy-start.15
  1045.2 2.0 copy-start.3
  1047.2 1.9 copy-start.14
Sparse Core Ops, SparseCore 0:
  14.7 61.0 all-reduce.7
  81.0 87.8 all-reduce.9
  330.4 107.8 all-reduce.11
  446.4 44.5 all-reduce.13
  665.3 362.7 all-reduce.15
where the time goes:
time: 1060 us
  waiting for transfers between devices  662 us (62%)
  other arithmetic  247 us (23%)
  matrix products  95.3 us (9%)
  local copies, waits for them, and re-layouts  35.5 us (3%)
  between operations  19.7 us (2%)
    psum x1, waiting for transfers between devices, per_device(): lax.psum((core_part, turn_left_part, turn_right_part), ('row', 'col'))  363 us
    another operation x29, other arithmetic, solve_rows(): factor = jnp.linalg.cholesky(gram)  162 us
    psum x1, waiting for transfers between devices, per_device(): right_image = lax.psum(right_part, 'row')  108 us
    psum x1, waiting for transfers between devices, per_device(): left_gram = lax.psum(gram_of(left_image), 'row')  87.5 us
    another operation x7, other arithmetic, solve_rows(): jax.scipy.linalg.solve_triangular(factor, image.T, lower=True)  81.5 us
    psum x1, waiting for transfers between devices, per_device(): lax.psum(jnp.dot(grad, right_old, preferred_element_type=jnp.float32), 'c...  61.2 us
    psum x1, waiting for transfers between devices, per_device(): right_gram = lax.psum(gram_of(right_image), 'col')  42.1 us
    another operation x14, matrix products, solve_rows(): jax.scipy.linalg.solve_triangular(factor, image.T, lower=True)  26.1 us
  transfers between devices with their start and end apart: 5, of which 5 were waited for; matrix products, arithmetic and copies ran while one was open for 0% of the time, Pallas kernels for 0%

commit v1 on v0

--- a/solution.py
+++ b/solution.py
@@ -51,7 +51,7 @@
         right_piece, right_prior, across, preferred_element_type=jnp.float32
     )
     core, turn_left, turn_right = lax.psum(
-        (core_part, turn_left_part, turn_right_part), ("row", "col")
+        lax.psum((core_part, turn_left_part, turn_right_part), "row"), "col"
     )
     core_upper, core_lower = split_pair(core)
     lifted_full = jnp.dot(left_basis, core_upper, preferred_element_type=jnp.float32) + jnp.dot(

time: 1060 us -> 881 us (0.83)
  waiting for transfers between devices: 662 us -> 476 us
    psum x1 -> x2, waiting for transfers between devices: 363 us -> 177 us  [the longest x1 101 us: per_device(): lax.psum((core_part, turn_left_part, turn_right_part), 'row')]
  transfers between devices with their start and end apart: 5 -> 6, of which waited for: 5 -> 6; matrix products, arithmetic and copies ran while one was open for 0% -> 0% of each run, Pallas kernels for 0% -> 0%
where the time goes in v1:
time: 881 us; the launch traced here: 875 us
  waiting for transfers between devices  476 us (54%)
  other arithmetic  247 us (28%)
  matrix products  95.2 us (11%)
  local copies, waits for them, and re-layouts  35.5 us (4%)
  between operations  20.2 us (2%)
    another operation x29, other arithmetic, solve_rows(): factor = jnp.linalg.cholesky(gram)  162 us
    psum x1, waiting for transfers between devices, per_device(): right_image = lax.psum(right_part, 'row')  108 us
    psum x1, waiting for transfers between devices, per_device(): lax.psum((core_part, turn_left_part, turn_right_part), 'row')  101 us
    psum x1, waiting for transfers between devices, per_device(): left_gram = lax.psum(gram_of(left_image), 'row')  87.5 us
    another operation x7, other arithmetic, solve_rows(): jax.scipy.linalg.solve_triangular(factor, image.T, lower=True)  81.5 us
    psum x1, waiting for transfers between devices, per_device(): lax.psum(lax.psum((core_part, turn_left_part, turn_right_part), 'row'), '...  76.6 us
    psum x1, waiting for transfers between devices, per_device(): lax.psum(jnp.dot(grad, right_old, preferred_element_type=jnp.float32), 'c...  61.2 us
    psum x1, waiting for transfers between devices, per_device(): right_gram = lax.psum(gram_of(right_image), 'col')  42.1 us
  transfers between devices with their start and end apart: 6, of which 6 were waited for; matrix products, arithmetic and copies ran while one was open for 0% of the time, Pallas kernels for 0%

profile of v1, /device:TPU:0, one launch (start us, length us, event | category | flops | bytes accessed | tf_op | source)
XLA Modules:
  0.0 875.4 jit_solution(5211227880351939616)
XLA Ops:
  7.2 1.5 copy-done
  8.8 5.8 fusion.102
  14.7 61.2 %all-reduce.10.cloned.1.call-done = f32[1024,512]{1,0:T(8,128)} async-done(((f32[1024,512]{1,0:T(8,128)}), f32[1024,512]{1,0:T(8,128)}) %all-reduce.10.cloned.1.call-update) | async-done | bytes 2097168 | tf_op jit(solution)/shard_map/psum | solution.py:25
  75.9 5.0 fusion.103
  81.4 87.5 %all-reduce.12.cloned.1.call-done = f32[512,512]{0,1:T(8,128)} async-done(((f32[512,512]{0,1:T(8,128)}), f32[512,512]{0,1:T(8,128)}) %all-reduce.12.cloned.1.call-update) | async-done | bytes 1048592 | tf_op jit(solution)/shard_map/psum | solution.py:26
  168.9 2.6 copy.11
  171.5 1.4 fusion.32
  174.0 11.7 %cholesky.286 = f32[128,128]{1,0:T(8,128)S(1)} custom-call(f32[128,128]{1,0:T(8,128)S(1)} %cholesky.426), custom_call_target="Cholesky" | custom-call | tf_op jit(solution)/shard_map/jit(cholesky)/cholesky | solution.py:8
  185.8 9.8 %custom-call.33 = f32[1,128,128]{1,2,0:T(8,128)S(1)} custom-call(f32[1,128,128]{2,1,0:T(8,128)S(1)} %get-tuple-element.68), custom_call_target="InvertDiagBlocksLowerTriangular" | custom-call | tf_op jit(solution)/shard_map/jit(cholesky)/cholesky | solution.py:8
  198.2 11.7 %cholesky.305 = f32[128,128]{1,0:T(8,128)S(1)} custom-call(f32[128,128]{1,0:T(8,128)S(1)} %cholesky.430), custom_call_target="Cholesky" | custom-call | tf_op jit(solution)/shard_map/jit(cholesky)/cholesky | solution.py:8
  209.9 10.0 %custom-call.34 = f32[1,128,128]{1,2,0:T(8,128)S(1)} custom-call(f32[1,128,128]{2,1,0:T(8,128)S(1)} %get-tuple-element.65), custom_call_target="InvertDiagBlocksLowerTriangular" | custom-call | tf_op jit(solution)/shard_map/jit(cholesky)/cholesky | solution.py:8
  220.2 1.3 convolution_subtract_fusion.7
  221.5 11.7 %cholesky.326 = f32[128,128]{1,0:T(8,128)S(1)} custom-call(f32[128,128]{1,0:T(8,128)S(1)} %cholesky.435), custom_call_target="Cholesky" | custom-call | tf_op jit(solution)/shard_map/jit(cholesky)/cholesky | solution.py:8
  233.2 9.8 %custom-call.35 = f32[1,128,128]{1,2,0:T(8,128)S(1)} custom-call(f32[1,128,128]{2,1,0:T(8,128)S(1)} %get-tuple-element.62), custom_call_target="InvertDiagBlocksLowerTriangular" | custom-call | tf_op jit(solution)/shard_map/jit(cholesky)/cholesky | solution.py:8
  244.5 11.7 %cholesky.343 = f32[128,128]{1,0:T(8,128)S(1)} custom-call(f32[128,128]{1,0:T(8,128)S(1)} %convolution_subtract_fusion.9), custom_call_target="Cholesky" | custom-call | tf_op jit(solution)/shard_map/jit(cholesky)/cholesky | solution.py:8
  260.7 1.5 select_select_fusion.1
  262.2 11.6 %while.2 = (s32[]{:T(128)}, f32[512,512]{1,0:T(8,128)}, s32[4,2]{0,1:T(2,128)S(1)}, f32[4,128,128]{2,1,0:T(8,128)S(1)}, s32[]{:T(128)}) while((s32[]{:T(128)}, f32[512,512]{1,0:T(8,128)}, s32[4,2]{0,1:T(2,128)S(1)}, f32[4,128,128]{2,1,0:T(8,128)S(1)}, s32[]{:T(128)}) %tuple.61), condition=%wide.while_cond, body=%wide.while_body.sunk | while | flops 2 | bytes 131189 | solution.py:9
  262.8 2.3 bitcast_dynamic-update-slice_fusion.4
  265.8 2.3 bitcast_dynamic-update-slice_fusion.4
  268.7 2.3 bitcast_dynamic-update-slice_fusion.4
  271.6 2.2 bitcast_dynamic-update-slice_fusion.4
  273.8 39.3 %custom-call.28 = f32[4,128,128]{1,2,0:T(8,128)S(1)} custom-call(f32[4,128,128]{2,1,0:T(8,128)S(1)} %get-tuple-element.12), custom_call_target="InvertDiagBlocksLowerTriangular" | custom-call | tf_op jit(solution)/shard_map/jit(_solve_triangular)/triangular_solve | solution.py:9
  313.1 1.8 fusion.98
  315.0 2.2 convolution_subtract_fusion.3
  317.8 2.8 convolution_subtract_fusion.2
  321.3 4.0 fusion.23
  326.0 4.4 convolution_bitcast_fusion
  330.5 108.0 %all-reduce.14.cloned.1.call-done = f32[2048,512]{0,1:T(8,128)} async-done(((f32[2048,512]{0,1:T(8,128)}), f32[2048,512]{0,1:T(8,128)}) %all-reduce.14.cloned.1.call-update) | async-done | bytes 4194320 | tf_op jit(solution)/shard_map/psum | solution.py:29
  438.5 7.9 fusion.104
  446.8 2.2 fusion.50
  449.0 42.1 %all-reduce.16.cloned.1.call-done = f32[512,512]{0,1:T(8,128)} async-done(((f32[512,512]{0,1:T(8,128)}), f32[512,512]{0,1:T(8,128)}) %all-reduce.16.cloned.1.call-update) | async-done | bytes 1048592 | tf_op jit(solution)/shard_map/psum | solution.py:30
  491.1 2.6 copy.13
  493.7 1.4 fusion.31
  496.1 11.7 %cholesky.358 = f32[128,128]{1,0:T(8,128)S(1)} custom-call(f32[128,128]{1,0:T(8,128)S(1)} %cholesky.439), custom_call_target="Cholesky" | custom-call | tf_op jit(solution)/shard_map/jit(cholesky)/cholesky | solution.py:8
  508.0 9.8 %custom-call.36 = f32[1,128,128]{1,2,0:T(8,128)S(1)} custom-call(f32[1,128,128]{2,1,0:T(8,128)S(1)} %get-tuple-element.58), custom_call_target="InvertDiagBlocksLowerTriangular" | custom-call | tf_op jit(solution)/shard_map/jit(cholesky)/cholesky | solution.py:8
  521.0 11.7 %cholesky.377 = f32[128,128]{1,0:T(8,128)S(1)} custom-call(f32[128,128]{1,0:T(8,128)S(1)} %cholesky.443), custom_call_target="Cholesky" | custom-call | tf_op jit(solution)/shard_map/jit(cholesky)/cholesky | solution.py:8
  532.8 10.2 %custom-call.37 = f32[1,128,128]{1,2,0:T(8,128)S(1)} custom-call(f32[1,128,128]{2,1,0:T(8,128)S(1)} %get-tuple-element.55), custom_call_target="InvertDiagBlocksLowerTriangular" | custom-call | tf_op jit(solution)/shard_map/jit(cholesky)/cholesky | solution.py:8
  544.2 1.3 convolution_subtract_fusion.6
  546.1 13.2 %cholesky.398 = f32[128,128]{1,0:T(8,128)} custom-call(f32[128,128]{1,0:T(8,128)} %cholesky.448), custom_call_target="Cholesky" | custom-call | tf_op jit(solution)/shard_map/jit(cholesky)/cholesky | solution.py:8
  559.3 1.5 select_reduce_fusion.1
  560.8 11.3 %custom-call.38 = f32[1,128,128]{1,2,0:T(8,128)} custom-call(f32[1,128,128]{2,1,0:T(8,128)} %get-tuple-element.52), custom_call_target="InvertDiagBlocksLowerTriangular" | custom-call | tf_op jit(solution)/shard_map/jit(cholesky)/cholesky | solution.py:8
  574.3 11.9 %cholesky.415 = f32[128,128]{1,0:T(8,128)S(1)} custom-call(f32[128,128]{1,0:T(8,128)S(1)} %convolution_subtract_fusion.8), custom_call_target="Cholesky" | custom-call | tf_op jit(solution)/shard_map/jit(cholesky)/cholesky | solution.py:8
  592.6 11.6 %while.3 = (s32[]{:T(128)}, f32[512,512]{1,0:T(8,128)}, s32[4,2]{0,1:T(2,128)S(1)}, f32[4,128,128]{2,1,0:T(8,128)S(1)}, s32[]{:T(128)}) while((s32[]{:T(128)}, f32[512,512]{1,0:T(8,128)}, s32[4,2]{0,1:T(2,128)S(1)}, f32[4,128,128]{2,1,0:T(8,128)S(1)}, s32[]{:T(128)}) %tuple.81), condition=%wide.while_cond.1, body=%wide.while_body.1.sunk | while | flops 2 | bytes 131189 | solution.py:9
  593.2 2.3 bitcast_dynamic-update-slice_fusion.5
  596.1 2.3 bitcast_dynamic-update-slice_fusion.5
  599.0 2.3 bitcast_dynamic-update-slice_fusion.5
  601.9 2.2 bitcast_dynamic-update-slice_fusion.5
  604.1 39.3 %custom-call.29 = f32[4,128,128]{1,2,0:T(8,128)S(1)} custom-call(f32[4,128,128]{2,1,0:T(8,128)S(1)} %get-tuple-element.20), custom_call_target="InvertDiagBlocksLowerTriangular" | custom-call | tf_op jit(solution)/shard_map/jit(_solve_triangular)/triangular_solve | solution.py:9
  643.5 2.3 fusion.101
  645.7 2.5 convolution_subtract_fusion.1
  649.3 2.3 convolution_subtract_fusion
  652.7 3.2 fusion.9
  657.7 1.6 copy-done.23
  659.4 2.4 fusion.1
  662.5 1.7 convolution_add_fusion.1
  664.2 1.3 fusion.47
  665.7 100.8 %all-reduce.18.cloned.1.call-done = (f32[512,512]{1,0:T(8,128)}, f32[512,512]{1,0:T(8,128)}, f32[512,512]{1,0:T(8,128)}) async-done(((f32[512,512]{1,0:T(8,128)}, f32[512,512]{1,0:T(8,128)}, f32[512,512]{1,0:T(8,128)}), (f32[512,512]{1,0:T(8,128)}, f32[512,512]{1,0:T(8,128)}, f32[512,512]{1,0:T(8,128)})) %all-reduce.18.cloned.1.call-update) | async-done | bytes 3145744 | tf_op jit(solution)/shard_map/psum | solution.py:54
  766.6 76.6 %all-reduce.20.cloned.1.call-done = (f32[512,512]{1,0:T(8,128)}, f32[512,512]{1,0:T(8,128)}, f32[512,512]{1,0:T(8,128)}) async-done(((f32[512,512]{1,0:T(8,128)}, f32[512,512]{1,0:T(8,128)}, f32[512,512]{1,0:T(8,128)}), (f32[512,512]{1,0:T(8,128)}, f32[512,512]{1,0:T(8,128)}, f32[512,512]{1,0:T(8,128)})) %all-reduce.20.cloned.1.call-update) | async-done | bytes 3145744 | tf_op jit(solution)/shard_map/psum | solution.py:53
  843.2 3.3 fusion.55
  846.5 10.6 %subtract_convert_fusion = bf16[1024,2048]{1,0:T(8,128)(2,1)} fusion(bf16[1024,2048]{1,0:T(8,128)(2,1)} %param.8, bf16[1024,2048]{1,0:T(8,128)(2,1)} %param.7, f32[1024,512]{1,0:T(8,128)} %fusion.55, f32[512,512]{1,0:T(8,128)} %get-tuple-element.40, bf16[128,2048]{1,0:T(8,128)(2,1)} %copy-done.10, bf16[128,2048]{1,0:T(8,128)(2,1)} %copy-done.13, ...), kind=kOutput, calls=%fused_computation.4 | convolution fusion | flops 2709520384 | bytes 18874368 | tf_op jit(solution)/shard_map/dot_general | solution.py:61
  857.2 3.2 fusion.105
  860.4 2.0 fusion.34
  862.4 1.9 fusion.106
  864.3 4.1 add_divide_fusion
  (124 shorter events, 32.2 us)
Async XLA Ops:
  7.2 1.6 copy-start
  7.2 68.7 %all-reduce.10.cloned.1.call-start = ((), (), s32[]{:S(2)}) async-start(), calls=%async_computation | async-start | bytes 4194304 | tf_op jit(solution)/shard_map/psum | solution.py:25
  14.6 154.3 %all-reduce.12.cloned.1.call-start = ((), (), s32[]{:S(2)}) async-start(), calls=%async_computation.1 | async-start | bytes 2097152 | tf_op jit(solution)/shard_map/psum | solution.py:26
  80.9 357.6 %all-reduce.14.cloned.1.call-start = ((), (), s32[]{:S(2)}) async-start(), calls=%async_computation.2 | async-start | bytes 8388608 | tf_op jit(solution)/shard_map/psum | solution.py:29
  168.9 2.6 copy-start.5
  173.0 1.0 copy-start.8
  313.1 4.7 copy-start.2
  315.0 131.7 %copy-start.16 = (bf16[128,1024]{1,0:T(8,128)(2,1)}, bf16[128,1024]{1,0:T(8,128)(2,1)S(1)}, u32[]{:S(2)}) copy-start(bf16[128,1024]{1,0:T(8,128)(2,1)S(1)} %get-tuple-element.75) | copy-start | bytes 786436
  317.8 128.8 %copy-start.18 = (bf16[128,1024]{1,0:T(8,128)(2,1)}, bf16[128,1024]{1,0:T(8,128)(2,1)S(1)}, u32[]{:S(2)}) copy-start(bf16[128,1024]{1,0:T(8,128)(2,1)S(1)} %get-tuple-element.73) | copy-start | bytes 786436
  320.7 5.3 copy-start.24
  321.3 125.4 %copy-start.20 = (bf16[128,1024]{1,0:T(8,128)(2,1)}, bf16[128,1024]{1,0:T(8,128)(2,1)S(1)}, u32[]{:S(2)}) copy-start(bf16[128,1024]{1,0:T(8,128)(2,1)S(1)} %get-tuple-element.71) | copy-start | bytes 786436
  330.4 160.7 %all-reduce.16.cloned.1.call-start = ((), (), s32[]{:S(2)}) async-start(), calls=%async_computation.3 | async-start | bytes 2097152 | tf_op jit(solution)/shard_map/psum | solution.py:30
  446.4 320.2 %all-reduce.18.cloned.1.call-start = ((), (), s32[]{:S(2)}) async-start(), calls=%async_computation.4 | async-start | bytes 6291456 | tf_op jit(solution)/shard_map/psum | solution.py:54
  491.1 2.6 copy-start.4
  495.2 1.0 copy-start.9
  520.4 0.7 copy-start.22
  645.7 11.5 %copy-start.11 = (bf16[128,2048]{1,0:T(8,128)(2,1)}, bf16[128,2048]{1,0:T(8,128)(2,1)S(1)}, u32[]{:S(2)}) copy-start(bf16[128,2048]{1,0:T(8,128)(2,1)S(1)} %get-tuple-element.83) | copy-start | bytes 1572868
  645.7 3.6 copy-start.1
  649.3 7.9 copy-start.12
  652.7 4.6 copy-start.13
  652.7 5.0 copy-start.25
  657.0 0.8 copy-start.10
  657.0 2.4 copy-start.23
  659.3 2.4 copy-start.17
  659.4 2.4 copy-start.19
  659.4 2.4 copy-start.21
  665.5 177.7 %all-reduce.20.cloned.1.call-start = ((), (), s32[]{:S(2)}) async-start(), calls=%async_computation.5 | async-start | bytes 6291456 | tf_op jit(solution)/shard_map/psum | solution.py:53
  846.5 10.6 %copy-start.6 = (f32[512,512]{1,0:T(8,128)S(1)}, f32[512,512]{1,0:T(8,128)}, u32[]{:S(2)}) copy-start(f32[512,512]{1,0:T(8,128)} %param.11) | copy-start | bytes 3145732
  857.1 3.2 copy-start.7
  857.1 3.2 copy-start.15
  860.4 2.0 copy-start.3
  862.4 1.9 copy-start.14
Sparse Core Ops, SparseCore 0:
  14.7 61.0 all-reduce.9
  81.0 87.8 all-reduce.11
  330.5 107.9 all-reduce.13
  446.5 44.5 all-reduce.15
  665.6 100.9 all-reduce.17
  769.0 74.2 all-reduce.19
